TPU v7x, 32 devices: a whole 2x2x4 slice. The times are simulated.
32 devices in a mesh: dp: 4 (over z), tensor: 8 (over y, x, core).
Axes of the slice: x: 2, y: 2, z: 4, core: 2. Of those that a mesh axis runs over, the one named last changes fastest.
Arguments:
- tokens: bfloat16 [8192, 1152], P('dp'), may hold values from -6 to 6
- condition: float32 [32, 1152], P('dp'), may hold values from -6 to 6
- timesteps: int32 [32], P('dp'), may hold values from 0 to 999
- route_masks: int32 [1000, 16, 2], P(None, 'tensor'), may hold values 0 or 1
- modulate_weight: bfloat16 [1152, 6, 1152], P(None, None, 'tensor'), may hold values from -0.1875 to 0.1875
- modulate_bias: bfloat16 [6, 1152], P(None, 'tensor'), may hold values from -1.5 to 1.5
- input_weight: bfloat16 [1152, 3, 1152], P(None, None, 'tensor'), may hold values from -0.1875 to 0.1875
- input_bias: bfloat16 [2, 1152], P(None, 'tensor'), may hold values from -1.5 to 1.5
- output_weight: bfloat16 [1152, 1152], P('tensor'), may hold values from -1.5 to 1.5
- output_bias: bfloat16 [1152], replicated, may hold values from -1.5 to 1.5
- expand_weight: bfloat16 [1152, 4608], P(None, 'tensor'), may hold values from -0.1875 to 0.1875
- expand_bias: bfloat16 [4608], P('tensor'), may hold values from -1.5 to 1.5
- reduce_weight: bfloat16 [4608, 1152], P('tensor'), may hold values from -0.1875 to 0.1875
- reduce_bias: bfloat16 [1152], replicated, may hold values from -1.5 to 1.5
- router_weight: bfloat16 [1152, 16, 2], P(None, 'tensor'), may hold values from -0.1875 to 0.1875
- router_bias: bfloat16 [16, 2], P('tensor'), may hold values from -1.2 to 1.2
- out_cotangent: bfloat16 [8192, 1152], P('dp'), may hold values from -6 to 6
Outputs:
- block_output: float32 [8192, 1152], P('dp')
- tokens_grad: float32 [8192, 1152], P('dp')
- modulate_weight_grad: float32 [1152, 6, 1152], P(None, None, 'tensor')
- modulate_bias_grad: float32 [6, 1152], P(None, 'tensor')
- input_weight_grad: float32 [1152, 3, 1152], P(None, None, 'tensor')
- input_bias_grad: float32 [2, 1152], P(None, 'tensor')
- output_weight_grad: float32 [1152, 1152], P('tensor')
- output_bias_grad: float32 [1152], replicated
- expand_weight_grad: float32 [1152, 4608], P(None, 'tensor')
- expand_bias_grad: float32 [4608], P('tensor')
- reduce_weight_grad: float32 [4608, 1152], P('tensor')
- reduce_bias_grad: float32 [1152], replicated
- router_weight_grad: float32 [1152, 16, 2], P(None, 'tensor')
- router_bias_grad: float32 [16, 2], P('tensor')
Inputs may be any that keep to these rules, and one draw needn't show every extreme that they name: `timesteps`: each timestep selects the row of route_masks used by its item.
All inputs are finite; a program needn't handle non-finite values. No bound on the sum of `route_masks` on one device may be relied on, other than what follows from the above.
Results may differ from a plain program's by a relative error of at most 0.013.
The roundings to bfloat16 on the way count: a program that leaves them out, or rounds other values in their place, can miss the bound.
Values may be sent and summed in bfloat16 or wider, within the bound.
A program may use at most 256 MiB of HBM per device.

v0:
```python
import math
import jax
import jax.numpy as jnp
from jax import lax
from jax.sharding import PartitionSpec as P

HIGHEST = lax.Precision.HIGHEST
EPSILON = 1e-06


def layer_norm(values):
    center = values - jnp.mean(values, axis=-1, keepdims=True)
    inverse = lax.rsqrt(jnp.mean(center * center, axis=-1, keepdims=True) + EPSILON)
    return (center * inverse, inverse)


def norm_back(grad_norm, normed, inverse):
    mean_grad = jnp.mean(grad_norm, axis=-1, keepdims=True)
    mean_cross = jnp.mean(grad_norm * normed, axis=-1, keepdims=True)
    return inverse * (grad_norm - mean_grad - normed * mean_cross)


def gelu_tanh(values):
    return jax.nn.gelu(values, approximate=True)


def contract_rows(left, right):
    return lax.dot_general(
        left, right, (((0,), (0,)), ((), ())), preferred_element_type=jnp.float32
    )


def contract_cols(left, right):
    return lax.dot_general(
        left, right, (((1,), (1,)), ((), ())), preferred_element_type=jnp.float32
    )


def body(
    tokens,
    condition,
    timesteps,
    route_masks,
    modulate_weight,
    modulate_bias,
    input_weight,
    input_bias,
    output_weight,
    output_bias,
    expand_weight,
    expand_bias,
    reduce_weight,
    reduce_bias,
    router_weight,
    router_bias,
    out_cotangent,
):
    model_width = tokens.shape[1]
    item_count = condition.shape[0]
    rows_all = tokens.shape[0]
    item_length = rows_all // item_count
    local_heads = router_weight.shape[1]
    local_width = input_weight.shape[2]
    head_size = local_width // local_heads
    group_width = expand_weight.shape[1] // local_heads
    score_scale = 1.0 / math.sqrt(head_size)
    silu_condition = jax.nn.silu(condition).astype(jnp.bfloat16)
    condition_low = condition.astype(jnp.bfloat16)
    modulate_part = jnp.einsum(
        "bd,dke->bke", silu_condition, modulate_weight, preferred_element_type=jnp.float32
    ) + modulate_bias.astype(jnp.float32)
    modulation = lax.all_gather(modulate_part, "tensor", axis=2, tiled=True)
    shift_one, scale_one, gate_one, shift_two, scale_two, gate_two = [
        modulation[:, column][:, None, :] for column in range(6)
    ]
    logits = jnp.einsum(
        "bd,dhc->bhc", condition_low, router_weight, preferred_element_type=jnp.float32
    ) + router_bias.astype(jnp.float32)
    sigmoid_out = jax.nn.sigmoid(logits)
    step_table = (
        timesteps[:, None] == jnp.arange(route_masks.shape[0], dtype=jnp.int32)[None, :]
    ).astype(jnp.float32)
    mask_rows = jnp.einsum(
        "bs,shc->bhc", step_table, route_masks.astype(jnp.float32), precision=HIGHEST
    )
    gate_values = mask_rows * sigmoid_out
    head_gate = gate_values[:, :, 0]
    group_gate = gate_values[:, :, 1]
    inputs_f = tokens.astype(jnp.float32).reshape(item_count, item_length, model_width)
    normed_one, inverse_one = layer_norm(inputs_f)
    hidden_one = (normed_one * (1.0 + scale_one) + shift_one).astype(jnp.bfloat16)
    projected = jnp.einsum(
        "bsd,dke->bske", hidden_one, input_weight, preferred_element_type=jnp.float32
    )
    input_bias_f = input_bias.astype(jnp.float32)
    head_shape = (item_count, item_length, local_heads, head_size)
    queries = (projected[:, :, 0] + input_bias_f[0]).astype(jnp.bfloat16).reshape(head_shape)
    keys_low = projected[:, :, 1].astype(jnp.bfloat16).reshape(head_shape)
    values_low = (projected[:, :, 2] + input_bias_f[1]).astype(jnp.bfloat16).reshape(head_shape)
    scores = (
        jnp.einsum("bqhe,bkhe->bhqk", queries, keys_low, preferred_element_type=jnp.float32)
        * score_scale
    )
    row_max = jnp.max(scores, axis=-1, keepdims=True)
    log_total = row_max + jnp.log(jnp.sum(jnp.exp(scores - row_max), axis=-1, keepdims=True))
    softmax_low = jnp.exp(scores - log_total).astype(jnp.bfloat16)
    mixed_heads = jnp.einsum(
        "bhqk,bkhe->bqhe", softmax_low, values_low, preferred_element_type=jnp.float32
    )
    gated_heads = (
        (mixed_heads * head_gate[:, None, :, None])
        .astype(jnp.bfloat16)
        .reshape(rows_all, local_width)
    )
    attention_part = jnp.dot(gated_heads, output_weight, preferred_element_type=jnp.float32)
    attention = (lax.psum(attention_part, "tensor") + output_bias.astype(jnp.float32)).reshape(
        item_count, item_length, model_width
    )
    residual_one = inputs_f + gate_one * attention
    normed_two, inverse_two = layer_norm(residual_one)
    hidden_two = (
        (normed_two * (1.0 + scale_two) + shift_two)
        .astype(jnp.bfloat16)
        .reshape(rows_all, model_width)
    )
    expanded = jnp.dot(
        hidden_two, expand_weight, preferred_element_type=jnp.float32
    ) + expand_bias.astype(jnp.float32)
    activated = gelu_tanh(expanded)
    group_shape = (item_count, item_length, local_heads, group_width)
    gated_channels = (
        (activated.reshape(group_shape) * group_gate[:, None, :, None])
        .astype(jnp.bfloat16)
        .reshape(rows_all, -1)
    )
    mlp_part = jnp.dot(gated_channels, reduce_weight, preferred_element_type=jnp.float32)
    branch_two = (lax.psum(mlp_part, "tensor") + reduce_bias.astype(jnp.float32)).reshape(
        item_count, item_length, model_width
    )
    block_output = residual_one + gate_two * branch_two
    cotangent = out_cotangent.astype(jnp.float32).reshape(item_count, item_length, model_width)
    gate_two_grad = jnp.sum(cotangent * branch_two, axis=1)
    branch_grad = (gate_two * cotangent).astype(jnp.bfloat16).reshape(rows_all, model_width)
    reduce_bias_grad = jnp.sum(branch_grad.astype(jnp.float32), axis=0)
    reduce_weight_grad = contract_rows(gated_channels, branch_grad)
    channel_blocks = contract_cols(branch_grad, reduce_weight).reshape(group_shape)
    group_gate_grad = jnp.sum(channel_blocks * activated.reshape(group_shape), axis=(1, 3))
    activated_grad = (channel_blocks * group_gate[:, None, :, None]).reshape(rows_all, -1)
    expanded_grad = jax.vjp(gelu_tanh, expanded)[1](activated_grad)[0].astype(jnp.bfloat16)
    expand_bias_grad = jnp.sum(expanded_grad.astype(jnp.float32), axis=0)
    expand_weight_grad = contract_rows(hidden_two, expanded_grad)
    hidden_two_part = contract_cols(expanded_grad, expand_weight)
    hidden_two_grad = lax.psum(hidden_two_part, "tensor").reshape(
        item_count, item_length, model_width
    )
    shift_two_grad = jnp.sum(hidden_two_grad, axis=1)
    scale_two_grad = jnp.sum(hidden_two_grad * normed_two, axis=1)
    residual_grad = cotangent + norm_back(
        hidden_two_grad * (1.0 + scale_two), normed_two, inverse_two
    )
    branch_one_grad = (gate_one * residual_grad).astype(jnp.bfloat16).reshape(rows_all, model_width)
    output_bias_grad = jnp.sum(branch_one_grad.astype(jnp.float32), axis=0)
    output_weight_grad = contract_rows(gated_heads, branch_one_grad)
    heads_grad = contract_cols(branch_one_grad, output_weight).reshape(head_shape)
    head_gate_grad = jnp.sum(heads_grad * mixed_heads, axis=(1, 3))
    mixed_grad = (heads_grad * head_gate[:, None, :, None]).astype(jnp.bfloat16)
    scores_again = (
        jnp.einsum("bqhe,bkhe->bhqk", queries, keys_low, preferred_element_type=jnp.float32)
        * score_scale
    )
    softmax_full = jnp.exp(scores_again - log_total)
    softmax_grad = jnp.einsum(
        "bqhe,bkhe->bhqk", mixed_grad, values_low, preferred_element_type=jnp.float32
    )
    values_grad = jnp.einsum(
        "bhqk,bqhe->bkhe",
        softmax_full.astype(jnp.bfloat16),
        mixed_grad,
        preferred_element_type=jnp.float32,
    )
    score_grad = (
        softmax_full * (softmax_grad - jnp.sum(softmax_grad * softmax_full, axis=-1, keepdims=True))
    ).astype(jnp.bfloat16)
    queries_grad = (
        jnp.einsum("bhqk,bkhe->bqhe", score_grad, keys_low, preferred_element_type=jnp.float32)
        * score_scale
    )
    keys_grad = (
        jnp.einsum("bhqk,bqhe->bkhe", score_grad, queries, preferred_element_type=jnp.float32)
        * score_scale
    )
    stacked_grad = (
        jnp.stack([queries_grad, keys_grad, values_grad], axis=2)
        .reshape(item_count, item_length, 3, local_width)
        .astype(jnp.bfloat16)
    )
    stacked_f = stacked_grad.astype(jnp.float32)
    input_bias_grad = jnp.stack(
        [jnp.sum(stacked_f[:, :, 0], axis=(0, 1)), jnp.sum(stacked_f[:, :, 2], axis=(0, 1))]
    )
    input_weight_grad = jnp.einsum(
        "bsd,bske->dke", hidden_one, stacked_grad, preferred_element_type=jnp.float32
    )
    hidden_one_part = jnp.einsum(
        "bske,dke->bsd", stacked_grad, input_weight, preferred_element_type=jnp.float32
    ).reshape(rows_all, model_width)
    hidden_one_grad = lax.psum(hidden_one_part, "tensor")
    gate_one_grad = jnp.sum(residual_grad * attention, axis=1)
    hidden_one_grad = hidden_one_grad.reshape(item_count, item_length, model_width)
    shift_one_grad = jnp.sum(hidden_one_grad, axis=1)
    scale_one_grad = jnp.sum(hidden_one_grad * normed_one, axis=1)
    tokens_grad = residual_grad + norm_back(
        hidden_one_grad * (1.0 + scale_one), normed_one, inverse_one
    )
    modulation_grad = jnp.stack(
        [
            shift_one_grad,
            scale_one_grad,
            gate_one_grad,
            shift_two_grad,
            scale_two_grad,
            gate_two_grad,
        ],
        axis=1,
    )
    column_start = lax.axis_index("tensor") * modulate_weight.shape[2]
    own_grad = lax.dynamic_slice_in_dim(modulation_grad, column_start, modulate_weight.shape[2], 2)
    modulate_weight_grad = jnp.einsum(
        "bd,bke->dke", silu_condition.astype(jnp.float32), own_grad, precision=HIGHEST
    )
    modulate_bias_grad = jnp.sum(own_grad, axis=0)
    gate_grad = jnp.stack([head_gate_grad, group_gate_grad], axis=-1)
    logit_grad = gate_grad * mask_rows * sigmoid_out * (1.0 - sigmoid_out)
    router_weight_grad = jnp.einsum(
        "bd,bhc->dhc", condition_low.astype(jnp.float32), logit_grad, precision=HIGHEST
    )
    router_bias_grad = jnp.sum(logit_grad, axis=0)
    summed = lax.psum(
        (
            modulate_weight_grad,
            modulate_bias_grad,
            input_weight_grad,
            input_bias_grad,
            output_weight_grad,
            output_bias_grad,
            expand_weight_grad,
            expand_bias_grad,
            reduce_weight_grad,
            reduce_bias_grad,
            router_weight_grad,
            router_bias_grad,
        ),
        "dp",
    )
    return (
        block_output.reshape(rows_all, model_width),
        tokens_grad.reshape(rows_all, model_width),
    ) + tuple(summed)


def solution(mesh):
    return jax.shard_map(
        body,
        mesh=mesh,
        in_specs=(
            P("dp", None),
            P("dp", None),
            P("dp"),
            P(None, "tensor", None),
            P(None, None, "tensor"),
            P(None, "tensor"),
            P(None, None, "tensor"),
            P(None, "tensor"),
            P("tensor", None),
            P(),
            P(None, "tensor"),
            P("tensor"),
            P("tensor", None),
            P(),
            P(None, "tensor", None),
            P("tensor", None),
            P("dp", None),
        ),
        out_specs=(
            P("dp", None),
            P("dp", None),
            P(None, None, "tensor"),
            P(None, "tensor"),
            P(None, None, "tensor"),
            P(None, "tensor"),
            P("tensor", None),
            P(),
            P(None, "tensor"),
            P("tensor"),
            P("tensor", None),
            P(),
            P(None, "tensor", None),
            P("tensor", None),
        ),
        check_vma=False,
    )
```

profile of v0, /device:TPU:0, one launch (start us, length us, event | category | flops | bytes accessed | tf_op | source)
XLA Modules:
  0.0 1134.2 jit_solution(17159783250025493048)
XLA Ops:
  15.8 29.1 %all_gather.3 = f32[8,6,1152]{1,0,2:T(8,128)} all-gather(f32[8,6,144]{1,0,2:T(8,128)S(1)} %copy.78), channel_id=1, replica_groups=mesh['dp'=4,'tensor'=8] {'tensor'}, dimensions={2}, use_global_device_ids=true | all-gather | bytes 248832 | tf_op jit(solution)/shard_map/all_gather | solution.py:72
  44.9 22.1 %fusion.64 = (f32[8,1,1152]{1,0,2:T(8,128)}, f32[8,1,1152]{1,0,2:T(8,128)}, f32[8,1,1152]{1,0,2:T(8,128)}, f32[8,1,1152]{1,0,2:T(8,128)}, f32[8,1,1152]{1,0,2:T(8,128)}, /*index=5*/f32[8,1,1152]{1,0,2:T(8,128)}) fusion(f32[8,6,1152]{1,0,2:T(8,128)} %all_gather.3), kind=kLoop, calls=%fused_computation.135 | loop fusion | bytes 442368 | tf_op jit(solution)/shard_map/slice | solution.py:74
  73.8 4.9 fusion.17
  84.7 5.3 fusion.70
  91.1 4.4 copy.121
  109.3 4.5 convert_reduce_fusion
  113.9 5.1 broadcast_multiply_fusion
  121.7 4.4 copy.122
  126.1 102.3 %all-reduce.8.cloned.1.call-done = f32[2048,1152]{1,0:T(8,128)} async-done(((f32[2048,1152]{1,0:T(8,128)}), f32[2048,1152]{1,0:T(8,128)}) %all-reduce.8.cloned.1.call-update) | async-done | bytes 9437200 | tf_op jit(solution)/shard_map/psum | solution.py:116
  228.4 10.4 fusion.62
  238.8 4.9 multiply_reduce_fusion.4
  248.4 8.9 multiply_convert_fusion
  258.6 7.0 fusion.72
  265.7 9.8 fusion.71
  275.6 128.3 %all-reduce.10.cloned.1.call-done = f32[2048,1152]{1,0:T(8,128)} async-done(((f32[2048,1152]{1,0:T(8,128)}), f32[2048,1152]{1,0:T(8,128)}) %all-reduce.10.cloned.1.call-update) | async-done | bytes 9437200 | tf_op jit(solution)/shard_map/psum | solution.py:153
  403.8 8.1 fusion.9
  412.9 10.7 convert_reduce_fusion.1
  434.7 5.4 convolution_bitcast_fusion
  440.8 7.9 fusion.75
  448.7 4.7 fusion.74
  453.5 4.3 fusion.73
  457.8 6.6 fusion.22
  464.4 215.9 %all-reduce.12.cloned.1.call-done = (f32[2048,1152]{1,0:T(8,128)}, f32[2048,1152]{1,0:T(8,128)}) async-done(((f32[2048,1152]{1,0:T(8,128)}, f32[2048,1152]{1,0:T(8,128)}), (f32[2048,1152]{1,0:T(8,128)}, f32[2048,1152]{1,0:T(8,128)})) %all-reduce.12.cloned.1.call-update) | async-done | bytes 18874384 | tf_op jit(solution)/shard_map/psum | solution.py:137
  680.3 22.4 %fusion.7 = (f32[8,1152]{1,0:T(8,128)S(1)}, f32[8,1152]{1,0:T(8,128)S(1)}, f32[8,1152]{1,0:T(8,128)S(1)}, f32[8,1152]{1,0:T(8,128)S(1)}, f32[8,1152]{1,0:T(8,128...) fusion(f32[2048,1152]{1,0:T(8,128)} %all-reduce.10.cloned.1.call-done, f32[2048,1152]{1,0:T(8,128)} %all-reduce.8.cloned.1.call-done, ...), kind=kLoop, calls=%fused_computation.17 | loop fusion | flops 61286400 | bytes 56976384 | tf_op jit(solution)/shard_map/reduce_sum | solution.py:157
  706.6 4.6 copy.123
  711.2 5.8 fusion.21
  719.3 7.0 fusion.8
  726.3 11.0 fusion.2
  737.4 11.9 %multiply_add_fusion = f32[2048,1152]{1,0:T(8,128)} fusion(f32[2048,1152]{1,0:T(8,128)} %get-tuple-element.52, f32[2048,1152]{1,0:T(8,128)} %get-tuple-element.31, bf16[2048,1152]{1,0:T(8,128)(2,1)} %param.17, f32[2048]{0:T(1024)S(1)} %broadcast_multiply_fusion.1, f32[2048]{0:T(1024)S(1)} %broadcast_multiply_fusion.2, f32[2048]{0:T(1024)S(1)} %copy-done.30, ...), kind=kLoop, calls=%fused_computation.24 | loop fusion | flops 21233664 | bytes 33099776 | tf_op jit(solution)/shard_map/add | solution.py:212
  749.4 26.8 %all-reduce.1 = (f32[6,144]{1,0:T(8,128)}, f32[2,144]{1,0:T(2,128)}, f32[1152]{0:T(1024)}, f32[576]{0:T(1024)}, f32[1152]{0:T(1024)}, /*index=5*/f32[1152,2,2]{0,2,1:T(2,128)}, f32[2,2]{1,0:T(2,128)}) all-reduce(f32[6,144]{1,0:T(8,128)S(1)} %dynamic-slice_reduce_fusion, ...), channel_id=1, replica_groups=mesh['dp'=4,'tensor'=8] {'dp'}, use_global_device_ids=true, to_apply=%region_23.24 | all-reduce | flops 8644 | bytes 69152 | tf_op jit(solution)/shard_map/psum | solution.py:238
  776.2 341.5 %all-reduce.14.cloned.1.call-done = (f32[1152,6,144]{0,2,1:T(8,128)}, f32[1152,3,144]{0,2,1:T(8,128)}, f32[144,1152]{1,0:T(8,128)}, f32[1152,576]{0,1:T(8,128)}, f32[576,1152]{1,0:T(8,128)}) async-done(((f32[1152,6,144]{0,2,1:T(8,128)}, f32[1152,3,144]{0,2,1:T(8,128)}, f32[144,1152]{1,0:T(8,128)}, f32[1152,576]{0,1:T(8,128)}, f32[576,1152]{1,0:T(8,128)}), (f32[1152,6,144]{0,2,1:T(8,128)}, ...) | async-done | bytes 11943952 | tf_op jit(solution)/shard_map/psum | solution.py:238
  1117.7 4.5 copy.141
  (211 shorter events, 68.9 us)
Async XLA Ops:
  7.2 7.6 copy-start
  7.2 7.0 copy-start.37
  7.2 7.6 copy-start.25
  7.2 221.2 %all-reduce.8.cloned.1.call-start = ((), (), s32[]{:S(2)}) async-start(), calls=%async_computation | async-start | bytes 18874368 | tf_op jit(solution)/shard_map/psum | solution.py:116
  10.4 34.5 %copy-start.27 = (f32[2048]{0:T(1024)}, f32[2048]{0:T(1024)S(1)}, u32[]{:S(2)}) copy-start(f32[2048]{0:T(1024)S(1)} %broadcast_multiply_fusion.6) | copy-start | bytes 24580
  67.0 6.8 copy-start.48
  84.6 5.4 copy-start.7
  90.0 313.8 %all-reduce.10.cloned.1.call-start = ((), (), s32[]{:S(2)}) async-start(), calls=%async_computation.1 | async-start | bytes 18874368 | tf_op jit(solution)/shard_map/psum | solution.py:153
  102.5 6.8 copy-start.23
  113.9 5.1 copy-start.11
  238.7 6.4 copy-start.2
  238.8 8.6 slice-start.2
  238.8 8.7 slice-start.4
  247.3 9.9 copy-start.13
  265.7 414.6 %all-reduce.12.cloned.1.call-start = ((), (), s32[]{:S(2)}) async-start(), calls=%async_computation.2 | async-start | bytes 37748736 | tf_op jit(solution)/shard_map/psum | solution.py:137
  403.8 9.1 copy-start.5
  412.9 10.7 copy-start.12
  440.1 8.6 slice-start
  440.1 677.6 %all-reduce.14.cloned.1.call-start = ((), (), s32[]{:S(2)}) async-start(), calls=%async_computation.3 | async-start | bytes 23887872 | tf_op jit(solution)/shard_map/psum | solution.py:238
  440.8 7.9 slice-start.1
  440.8 7.9 copy-start.54
  680.3 22.5 %copy-start.26 = (f32[8,1152]{1,0:T(8,128)S(1)}, f32[8,1152]{1,0:T(8,128)}, u32[]{:S(2)}) copy-start(f32[8,1152]{1,0:T(8,128)} %param.18) | copy-start | bytes 110596
  711.1 6.0 copy-start.32
  711.1 7.9 copy-start.43
  711.1 7.9 copy-start.44
  711.2 8.1 copy-start.28
  711.2 8.1 copy-start.30
  719.3 7.0 copy-start.24
  737.3 12.0 %copy-start.31 = (f32[1152]{0:T(1024)S(1)}, f32[1152]{0:T(1024)}, u32[]{:S(2)}) copy-start(f32[1152]{0:T(1024)} %get-tuple-element.46) | copy-start | bytes 13828
  737.3 12.0 %copy-start.40 = (f32[576]{0:T(1024)S(1)}, f32[576]{0:T(1024)}, u32[]{:S(2)}) copy-start(f32[576]{0:T(1024)} %get-tuple-element.58) | copy-start | bytes 6916
  1117.7 5.8 copy-start.22
  1117.7 6.6 copy-start.15
  (34 other events, 84.1 us)
Sparse Core Ops, SparseCore 0:
  90.1 138.1 all-reduce.7
  265.8 137.9 all-reduce.9
  440.2 240.0 all-reduce.11
  706.7 410.9 all-reduce.13
where the time goes:
time: 1140 us; the launch traced here: 1130 us
  waiting for transfers between devices  788 us (69%)
  other arithmetic  112 us (10%)
  matrix products  84.5 us (7%)
  local copies, waits for them, and re-layouts  78.5 us (7%)
  blocking collectives  55.9 us (5%)
  between operations  14.9 us (1%)
    psum x1, waiting for transfers between devices, body(): lax.psum((modulate_weight_grad, modulate_bias_grad, input_weight_grad, in...  341 us
    psum x1, waiting for transfers between devices, body(): lax.psum(mlp_part, 'tensor') + reduce_bias.astype(jnp.float32)  216 us
    psum x1, waiting for transfers between devices, body(): lax.psum(hidden_two_part, 'tensor')  128 us
    psum x1, waiting for transfers between devices, body(): lax.psum(attention_part, 'tensor') + output_bias.astype(jnp.float32)  102 us
    unnamed x144, local copies, waits for them, and re-layouts  51.7 us
    all_gather x1, blocking collectives, body(): modulation = lax.all_gather(modulate_part, 'tensor', axis=2, tiled=True)  29.1 us
    psum x1, blocking collectives, body(): lax.psum((modulate_weight_grad, modulate_bias_grad, input_weight_grad, in...  26.8 us
  transfers between devices with their start and end apart: 4, of which 4 were waited for; matrix products, arithmetic and copies ran while one was open for 10% of the time, Pallas kernels for 0%

commit v1 on v0

--- a/solution.py
+++ b/solution.py
@@ -69,7 +69,16 @@
     modulate_part = jnp.einsum(
         "bd,dke->bke", silu_condition, modulate_weight, preferred_element_type=jnp.float32
     ) + modulate_bias.astype(jnp.float32)
-    modulation = lax.all_gather(modulate_part, "tensor", axis=2, tiled=True)
+    out_arr = lax.axis_size("tensor")
+    p_next = lax.axis_index("tensor")
+    part_now, built, w2 = (out_arr, p_next, modulate_part.shape[2])
+    formed, outcome_arr = (modulate_part, 1)
+    while outcome_arr < part_now:
+        last = tuple(((it, (it - outcome_arr) % part_now) for it in range(part_now)))
+        h_now = lax.ppermute(formed, axis_name="tensor", perm=last)
+        formed = jnp.concatenate([formed, h_now], 2)
+        outcome_arr = 2 * outcome_arr
+    modulation = jnp.roll(formed, built * w2, 2)
     shift_one, scale_one, gate_one, shift_two, scale_two, gate_two = [
         modulation[:, column][:, None, :] for column in range(6)
     ]

time: 1140 us -> 1100 us (0.965)
  local copies, waits for them, and re-layouts: 78.5 us -> 40.6 us
  blocking collectives: 55.9 us -> 24.9 us
  waiting for transfers between devices: 788 us -> 818 us
  other arithmetic: 112 us -> 100 us
    all_gather x1 -> x0, blocking collectives: 29.1 us -> none  [body(): modulation = lax.all_gather(modulate_part, 'tensor', axis=2, tiled=True)]
    slice x1 -> x0, local copies, waits for them, and re-layouts: 22.1 us -> none  [body(): modulation[:, column][:, None, :]]
    psum x1, waiting for transfers between devices: 102 us -> 119 us  [body(): lax.psum(attention_part, 'tensor') + output_bias.astype(jnp.float32)]
    unnamed x144 -> x160, local copies, waits for them, and re-layouts: 51.7 us -> 36.1 us
  transfers between devices with their start and end apart: 4 -> 7, of which waited for: 4 -> 6; matrix products, arithmetic and copies ran while one was open for 10% -> 9% of each run, Pallas kernels for 0% -> 0%
where the time goes in v1:
time: 1100 us; the launch traced here: 1090 us
  waiting for transfers between devices  818 us (74%)
  other arithmetic  100 us (9%)
  matrix products  85.4 us (8%)
  local copies, waits for them, and re-layouts  40.6 us (4%)
  blocking collectives  24.9 us (2%)
  between operations  15.1 us (1%)
    psum x1, waiting for transfers between devices, body(): lax.psum((modulate_weight_grad, modulate_bias_grad, input_weight_grad, in...  347 us
    psum x1, waiting for transfers between devices, body(): lax.psum(mlp_part, 'tensor') + reduce_bias.astype(jnp.float32)  216 us
    psum x1, waiting for transfers between devices, body(): lax.psum(hidden_two_part, 'tensor')  128 us
    psum x1, waiting for transfers between devices, body(): lax.psum(attention_part, 'tensor') + output_bias.astype(jnp.float32)  119 us
    unnamed x160, local copies, waits for them, and re-layouts  36.1 us
    psum x1, blocking collectives, body(): lax.psum((modulate_weight_grad, modulate_bias_grad, input_weight_grad, in...  24.9 us
    reduce_sum x2, other arithmetic, norm_back(): mean_grad = jnp.mean(grad_norm, axis=-1, keepdims=True)  24 us
    reduce_sum x1, other arithmetic, body(): scale_two_grad = jnp.sum(hidden_two_grad * normed_two, axis=1)  22.4 us
  transfers between devices with their start and end apart: 7, of which 6 were waited for; matrix products, arithmetic and copies ran while one was open for 9% of the time, Pallas kernels for 0%

profile of v1, /device:TPU:0, one launch (start us, length us, event | category | flops | bytes accessed | tf_op | source)
XLA Modules:
  0.0 1089.6 jit_solution(335831073917692594)
XLA Ops:
  10.6 3.3 collective-permute-start
  20.9 3.7 collective-permute-done.1
  25.6 4.1 collective-permute-done.2
  30.1 4.8 fusion.17
  39.1 5.3 fusion.71
  45.7 4.5 copy.86
  52.3 4.9 broadcast_multiply_fusion
  60.0 4.4 copy.87
  64.3 118.9 %all-reduce.8.cloned.1.call-done = f32[2048,1152]{1,0:T(8,128)} async-done(((f32[2048,1152]{1,0:T(8,128)}), f32[2048,1152]{1,0:T(8,128)}) %all-reduce.8.cloned.1.call-update) | async-done | bytes 9437200 | tf_op jit(solution)/shard_map/psum | solution.py:125
  183.2 10.4 fusion.64
  193.6 4.9 multiply_reduce_fusion.4
  203.6 9.3 multiply_convert_fusion
  214.3 6.6 fusion.73
  221.0 10.0 fusion.72
  230.9 128.1 %all-reduce.10.cloned.1.call-done = f32[2048,1152]{1,0:T(8,128)} async-done(((f32[2048,1152]{1,0:T(8,128)}), f32[2048,1152]{1,0:T(8,128)}) %all-reduce.10.cloned.1.call-update) | async-done | bytes 9437200 | tf_op jit(solution)/shard_map/psum | solution.py:162
  359.1 8.1 fusion.9
  368.2 10.7 convert_reduce_fusion.1
  390.0 5.3 convolution_bitcast_fusion
  396.0 7.9 fusion.76
  404.0 4.7 fusion.75
  408.8 4.3 fusion.74
  413.1 6.6 fusion.22
  419.7 215.8 %all-reduce.12.cloned.1.call-done = (f32[2048,1152]{1,0:T(8,128)}, f32[2048,1152]{1,0:T(8,128)}) async-done(((f32[2048,1152]{1,0:T(8,128)}, f32[2048,1152]{1,0:T(8,128)}), (f32[2048,1152]{1,0:T(8,128)}, f32[2048,1152]{1,0:T(8,128)})) %all-reduce.12.cloned.1.call-update) | async-done | bytes 18874384 | tf_op jit(solution)/shard_map/psum | solution.py:146
  635.5 22.4 %fusion.7 = (f32[8,1152]{1,0:T(8,128)S(1)}, f32[8,1152]{1,0:T(8,128)S(1)}, f32[8,1152]{1,0:T(8,128)S(1)}, f32[8,1152]{1,0:T(8,128)S(1)}, f32[8,1152]{1,0:T(8,128...) fusion(f32[2048,1152]{1,0:T(8,128)} %all-reduce.10.cloned.1.call-done, f32[2048,1152]{1,0:T(8,128)} %all-reduce.8.cloned.1.call-done, ...), kind=kLoop, calls=%fused_computation.17 | loop fusion | flops 61286400 | bytes 56976384 | tf_op jit(solution)/shard_map/reduce_sum | solution.py:166
  658.0 3.8 fusion.37
  661.8 4.6 copy.88
  666.4 5.8 fusion.21
  674.6 15.9 %fusion.8 = (f32[2048]{0:T(1024)S(1)}, f32[2048]{0:T(1024)S(1)}, f32[2048,1152]{1,0:T(8,128)}) fusion(f32[2048,1152]{1,0:T(8,128)} %get-tuple-element.31, f32[8,1152]{1,0:T(8,128)S(1)} %get-tuple-element.67, f32[2048]{0:T(1024)S(1)} %copy-done.29, f32[2048]{0:T(1024)S(1)} %copy-done.27, bf16[2048,1152]{1,0:T(8,128)(2,1)} %param.17, ...), kind=kLoop, calls=%fused_computation.34 | loop fusion | flops 21229568 | bytes 42573824 | tf_op jit(solution)/shard_map/reduce_sum | solution.py:18
  695.2 5.3 multiply_add_fusion
  700.6 24.9 %all-reduce.1 = (f32[6,144]{1,0:T(8,128)}, f32[2,144]{1,0:T(2,128)}, f32[1152]{0:T(1024)}, f32[576]{0:T(1024)}, f32[1152]{0:T(1024)}, /*index=5*/f32[1152,2,2]{0,2,1:T(2,128)}, f32[2,2]{1,0:T(2,128)}) all-reduce(f32[6,144]{1,0:T(8,128)S(1)} %dynamic-slice_reduce_fusion, ...), channel_id=1, replica_groups=mesh['dp'=4,'tensor'=8] {'dp'}, use_global_device_ids=true, to_apply=%region_23.24 | all-reduce | flops 8644 | bytes 69152 | tf_op jit(solution)/shard_map/psum | solution.py:247
  725.6 347.4 %all-reduce.14.cloned.1.call-done = (f32[1152,6,144]{0,2,1:T(8,128)}, f32[1152,3,144]{0,2,1:T(8,128)}, f32[144,1152]{1,0:T(8,128)}, f32[1152,576]{0,1:T(8,128)}, f32[576,1152]{1,0:T(8,128)}) async-done(((f32[1152,6,144]{0,2,1:T(8,128)}, f32[1152,3,144]{0,2,1:T(8,128)}, f32[144,1152]{1,0:T(8,128)}, f32[1152,576]{0,1:T(8,128)}, f32[576,1152]{1,0:T(8,128)}), (f32[1152,6,144]{0,2,1:T(8,128)}, ...) | async-done | bytes 11943952 | tf_op jit(solution)/shard_map/psum | solution.py:247
  1073.0 4.5 copy.106
  (236 shorter events, 53.3 us)
Async XLA Ops:
  7.2 176.0 %all-reduce.8.cloned.1.call-start = ((), (), s32[]{:S(2)}) async-start(), calls=%async_computation | async-start | bytes 18874368 | tf_op jit(solution)/shard_map/psum | solution.py:125
  7.2 10.5 copy-start.3
  10.6 9.6 collective-permute-start
  14.6 15.5 %copy-start.50 = (bf16[1152,3,144]{0,2,1:T(8,128)(2,1)S(1)}, bf16[1152,3,144]{0,2,1:T(8,128)(2,1)}, u32[]{:S(2)}) copy-start(bf16[1152,3,144]{0,2,1:T(8,128)(2,1)} %param.23) | copy-start | bytes 2985988
  20.2 4.4 collective-permute-start.1
  20.9 14.0 %copy-start.31 = (f32[8,256]{1,0:T(8,128)}, f32[8,256]{1,0:T(8,128)S(1)}, u32[]{:S(2)}) copy-start(f32[8,256]{1,0:T(8,128)S(1)} %div.41) | copy-start | bytes 24580
  24.7 4.9 collective-permute-start.2
  25.4 11.4 %copy-start.38 = (f32[2,72]{1,0:T(2,128)}, f32[2,72]{1,0:T(2,128)S(1)}, u32[]{:S(2)}) copy-start(f32[2,72]{1,0:T(2,128)S(1)} %add.219) | copy-start | bytes 1732
  25.5 9.7 copy-start.36
  25.6 9.3 copy-start.33
  44.5 314.6 %all-reduce.10.cloned.1.call-start = ((), (), s32[]{:S(2)}) async-start(), calls=%async_computation.1 | async-start | bytes 18874368 | tf_op jit(solution)/shard_map/psum | solution.py:162
  193.6 8.6 slice-start.12
  193.6 8.7 slice-start.14
  202.1 10.7 copy-start.14
  220.9 414.6 %all-reduce.12.cloned.1.call-start = ((), (), s32[]{:S(2)}) async-start(), calls=%async_computation.2 | async-start | bytes 37748736 | tf_op jit(solution)/shard_map/psum | solution.py:146
  359.1 9.1 copy-start.6
  368.2 10.7 copy-start.13
  395.3 8.6 slice-start.10
  395.3 677.6 %all-reduce.14.cloned.1.call-start = ((), (), s32[]{:S(2)}) async-start(), calls=%async_computation.3 | async-start | bytes 23887872 | tf_op jit(solution)/shard_map/psum | solution.py:247
  396.0 7.9 slice-start.11
  396.0 7.9 copy-start.55
  635.5 22.4 %copy-start.25 = (f32[8,1152]{1,0:T(8,128)S(1)}, f32[8,1152]{1,0:T(8,128)}, u32[]{:S(2)}) copy-start(f32[8,1152]{1,0:T(8,128)} %param.18) | copy-start | bytes 110596
  666.4 8.2 copy-start.27
  666.4 8.2 copy-start.29
  666.4 24.1 %slice-start = ((s8[4718592]{0:T(1024)(128)(4,1)}), s8[524288]{0:T(1024)(128)(4,1)S(1)}, s32[]{:S(2)}) async-start(s8[4718592]{0:T(1024)(128)(4,1)} %bitcast.215), calls=%async_computation.4 | async-start | bytes 1048576
  674.6 16.0 %slice-start.2 = ((s8[9437184]{0:T(1024)(128)(4,1)}), s8[4194304]{0:T(1024)(128)(4,1)S(1)}, s32[]{:S(2)}) async-start(s8[9437184]{0:T(1024)(128)(4,1)} %bitcast.217), calls=%async_computation.6 | async-start | bytes 8388608
  674.6 16.0 %slice-start.7 = ((s8[9437184]{0:T(1024)(128)(4,1)}), s8[4194304]{0:T(1024)(128)(4,1)S(1)}, s32[]{:S(2)}) async-start(s8[9437184]{0:T(1024)(128)(4,1)} %bitcast.222), calls=%async_computation.11 | async-start | bytes 8388608
  674.6 17.7 %slice-start.1 = ((s8[4718592]{0:T(1024)(128)(4,1)}), s8[4194304]{0:T(1024)(128)(4,1)S(1)}, s32[]{:S(2)}) async-start(s8[4718592]{0:T(1024)(128)(4,1)} %bitcast.215), calls=%async_computation.5 | async-start | bytes 8388608
  674.6 18.8 %slice-start.3 = ((s8[9437184]{0:T(1024)(128)(4,1)}), s8[4194304]{0:T(1024)(128)(4,1)S(1)}, s32[]{:S(2)}) async-start(s8[9437184]{0:T(1024)(128)(4,1)} %bitcast.217), calls=%async_computation.7 | async-start | bytes 8388608
  674.6 19.1 %slice-start.4 = ((s8[9437184]{0:T(1024)(128)(4,1)}), s8[1048576]{0:T(1024)(128)(4,1)S(1)}, s32[]{:S(2)}) async-start(s8[9437184]{0:T(1024)(128)(4,1)} %bitcast.217), calls=%async_computation.8 | async-start | bytes 2097152
  674.6 20.3 %slice-start.8 = ((s8[9437184]{0:T(1024)(128)(4,1)}), s8[4194304]{0:T(1024)(128)(4,1)S(1)}, s32[]{:S(2)}) async-start(s8[9437184]{0:T(1024)(128)(4,1)} %bitcast.222), calls=%async_computation.12 | async-start | bytes 8388608
  674.6 20.5 %slice-start.9 = ((s8[9437184]{0:T(1024)(128)(4,1)}), s8[1048576]{0:T(1024)(128)(4,1)S(1)}, s32[]{:S(2)}) async-start(s8[9437184]{0:T(1024)(128)(4,1)} %bitcast.222), calls=%async_computation.13 | async-start | bytes 2097152
  (48 other events, 190.7 us)
Sparse Core Ops, SparseCore 0:
  44.6 138.5 all-reduce.7
  221.1 137.9 all-reduce.9
  395.5 239.9 all-reduce.11
  661.9 410.9 all-reduce.13
